TPU v7x, 512 devices: a whole 4x8x8 slice. The times are simulated.
512 devices in a mesh: region: 16 (over y, core), var: 32 (over z, x).
Axes of the slice: x: 4, y: 8, z: 8, core: 2. Of those that a mesh axis runs over, the one named last changes fastest.
Arguments:
- state: float32 [262144, 768], P(('region', 'var')), may hold values from -6 to 6
- taper: bfloat16 [4, 262144, 384], P(None, ('region', 'var')), may hold values from 0.19921875 to 1
- block_mask: int32 [4, 2048, 3], P(None, ('region', 'var')), may hold values 0 or 1
- anom_fly: float32 [16, 384, 768], P('region', 'var'), may hold values from -6 to 6
- incr_fly: float32 [16, 384, 768], P('region', 'var'), may hold values from -6 to 6
- anom_new: float32 [3, 384, 768], P(None, 'var'), may hold values from -6 to 6
- incr_new: float32 [3, 384, 768], P(None, 'var'), may hold values from -6 to 6
Outputs:
- updated: float32 [262144, 768], P(('region', 'var'))
All inputs are finite; a program needn't handle non-finite values. No bound on the sum of `block_mask` on one device may be relied on, other than what follows from the above.
Results may differ from a plain program's by a relative error of at most 0.0003.
Values sent between devices are 32-bit elements; how exact they have to be, the bound alone decides.
No kernel may reach another device: no remote copies, remote signals or barrier semaphores. Data moves between devices by JAX's collectives and lax.ppermute only.
A program may use at most 64 MiB of HBM per device.

v0:
```python
import jax
import jax.numpy as jnp
from jax import lax
from jax.sharding import PartitionSpec as P

MEMBERS = 768
BLOCK = 128
TICKS = 4


def shifted(block, axis, distance):
    devices = range(lax.axis_size(axis))
    route = [(i - distance, i) for i in devices if i - distance in devices]
    return lax.ppermute(block, axis, route)


def localizer(taper_now, block_flags):
    row_blocks, obs_blocks = block_flags.shape
    expanded = jnp.broadcast_to(
        block_flags[:, None, :, None], (row_blocks, BLOCK, obs_blocks, BLOCK)
    )
    expanded = expanded.reshape(row_blocks * BLOCK, obs_blocks * BLOCK).astype(jnp.float32)
    return taper_now.astype(jnp.float32) * expanded


def assimilate(state_rows, taper_now, block_flags, batch_pair):
    localize = localizer(taper_now, block_flags)
    gathered = lax.all_gather(batch_pair, "var", axis=1, tiled=True)
    covar = lax.dot_general(
        state_rows,
        gathered[0],
        (((1,), (1,)), ((), ())),
        precision=lax.Precision.HIGHEST,
        preferred_element_type=jnp.float32,
    )
    weights = localize * covar / (MEMBERS - 1)
    increment = jnp.dot(
        weights, gathered[1], precision=lax.Precision.HIGHEST, preferred_element_type=jnp.float32
    )
    return state_rows + increment


def on_device(state, taper, block_mask, anom_fly, incr_fly, anom_new, incr_new):
    region_id = lax.axis_index("region")
    in_flight = jnp.stack([anom_fly[0], incr_fly[0]])
    entering = jnp.stack([anom_new, incr_new], 1)
    state_rows = state
    batch_pair = in_flight
    for tick_num in range(TICKS):
        if tick_num > 0:
            arrived = shifted(batch_pair, "region", 1)
            batch_pair = jnp.where(region_id == 0, entering[tick_num - 1], arrived)
        state_rows = assimilate(state_rows, taper[tick_num], block_mask[tick_num], batch_pair)
    return state_rows


def solution(mesh):
    in_specs = (
        P(("region", "var"), None),
        P(None, ("region", "var"), None),
        P(None, ("region", "var"), None),
        P("region", "var", None),
        P("region", "var", None),
        P(None, "var", None),
        P(None, "var", None),
    )
    out_specs = P(("region", "var"), None)
    return jax.shard_map(
        on_device, mesh=mesh, in_specs=in_specs, out_specs=out_specs, check_vma=False
    )
```

profile of v0, /device:TPU:8, one launch (start us, length us, event | category | flops | bytes accessed | tf_op | source)
XLA Modules:
  0.0 368.7 jit_solution(4278995919764913455)
XLA Ops:
  6.5 0.0 copy-start.1
  6.5 0.0 all-gather.5.cloned.1.call-start
  6.5 1.6 pad_maximum_fusion.1
  8.1 0.0 all-gather.5.cloned.1.call-update
  8.2 0.0 all-gather.7.cloned.1.call-start
  8.2 1.9 collective-permute-start
  10.1 1.0 stack.13
  11.1 1.0 stack.14
  12.1 2.0 collective-permute-done
  14.1 0.7 bitcast_select_fusion.1
  14.8 0.0 all-gather.7.cloned.1.call-update
  14.8 0.0 all-gather.9.cloned.1.call-start
  14.9 1.9 collective-permute-start.1
  16.8 4.5 %collective-permute-done.1 = f32[2,12,768]{2,0,1:T(2,128)S(1)} collective-permute-done((f32[2,12,768]{2,0,1:T(2,128)}, f32[2,12,768]{2,0,1:T(2,128)S(1)}, u32[]{:S(2)}, u32[]{:S(2)}) %collective-permute-start.1) | collective-permute-done | bytes 73760 | tf_op jit(solution)/shard_map/ppermute | solution.py:14
  21.3 0.7 bitcast_select_fusion
  22.0 0.0 all-gather.9.cloned.1.call-update
  22.0 0.0 all-gather.11.cloned.1.call-start
  22.1 1.9 collective-permute-start.2
  24.0 4.0 %collective-permute-done.2 = f32[2,12,768]{2,0,1:T(2,128)S(1)} collective-permute-done((f32[2,12,768]{2,0,1:T(2,128)}, f32[2,12,768]{2,0,1:T(2,128)S(1)}, u32[]{:S(2)}, u32[]{:S(2)}) %collective-permute-start.2) | collective-permute-done | bytes 73760 | tf_op jit(solution)/shard_map/ppermute | solution.py:14
  28.0 0.7 fusion.24
  28.7 0.0 all-gather.11.cloned.1.call-update
  28.7 0.0 copy-done.1
  28.7 0.0 copy-start.3
  28.7 0.2 fusion.29
  28.9 0.2 copy.73
  29.1 0.3 copy-done.3
  29.4 0.1 copy.74
  29.5 0.1 copy.49
  29.6 0.2 copy.75
  29.8 0.1 copy.76
  29.9 0.1 copy.52
  30.0 0.9 copy.77
  31.0 0.1 copy.78
  31.1 0.1 copy.56
  31.1 0.2 copy.79
  31.4 0.1 copy.80
  31.5 0.1 copy.60
  31.5 67.4 %all-gather.5.cloned.1.call-done = f32[2,384,768]{2,0,1:T(2,128)} async-done(((f32[2,12,768]{2,0,1:T(2,128)}), f32[2,384,768]{2,0,1:T(2,128)}) %all-gather.5.cloned.1.call-update) | async-done | bytes 2359312 | tf_op jit(solution)/shard_map/all_gather | solution.py:28
  99.0 0.0 copy-start
  99.0 4.5 %fusion.28 = (f32[1,384,768]{2,0,1:T(1,128)S(1)}, f32[1,384,768]{2,0,1:T(1,128)S(1)}) fusion(f32[2,384,768]{2,0,1:T(2,128)} %all-gather.5.cloned.1.call-done), kind=kLoop, calls=%fused_computation.52 | loop fusion | bytes 4718592 | tf_op jit(solution)/shard_map/slice | solution.py:38
  103.5 0.2 broadcast_in_dim.8
  103.7 0.0 copy-done
  103.7 2.1 fusion.1
  105.8 2.9 convolution_add_fusion.3
  108.7 74.4 %all-gather.7.cloned.1.call-done = f32[2,384,768]{2,0,1:T(2,128)} async-done(((f32[2,12,768]{2,0,1:T(2,128)}), f32[2,384,768]{2,0,1:T(2,128)}) %all-gather.7.cloned.1.call-update) | async-done | bytes 2359312 | tf_op jit(solution)/shard_map/all_gather | solution.py:28
  183.1 4.4 %fusion.27 = (f32[1,384,768]{2,0,1:T(1,128)S(1)}, f32[1,384,768]{2,0,1:T(1,128)S(1)}) fusion(f32[2,384,768]{2,0,1:T(2,128)} %all-gather.7.cloned.1.call-done), kind=kLoop, calls=%fused_computation.51 | loop fusion | bytes 4718592 | tf_op jit(solution)/shard_map/slice | solution.py:38
  187.5 0.2 broadcast_in_dim.9
  187.7 2.3 fusion.2
  190.1 2.8 convolution_add_fusion.2
  192.9 0.0 copy-start.2
  192.9 74.4 %all-gather.9.cloned.1.call-done = f32[2,384,768]{2,0,1:T(2,128)} async-done(((f32[2,12,768]{2,0,1:T(2,128)}), f32[2,384,768]{2,0,1:T(2,128)}) %all-gather.9.cloned.1.call-update) | async-done | bytes 2359312 | tf_op jit(solution)/shard_map/all_gather | solution.py:28
  267.3 4.4 %fusion.26 = (f32[1,384,768]{2,0,1:T(1,128)S(1)}, f32[1,384,768]{2,0,1:T(1,128)S(1)}) fusion(f32[2,384,768]{2,0,1:T(2,128)} %all-gather.9.cloned.1.call-done), kind=kLoop, calls=%fused_computation.50 | loop fusion | bytes 4718592 | tf_op jit(solution)/shard_map/slice | solution.py:38
  271.7 0.2 broadcast_in_dim.10
  271.9 0.0 copy-done.2
  271.9 2.1 fusion.3
  274.0 2.8 convolution_add_fusion.1
  276.8 74.5 %all-gather.11.cloned.1.call-done = f32[2,384,768]{2,0,1:T(2,128)} async-done(((f32[2,12,768]{2,0,1:T(2,128)}), f32[2,384,768]{2,0,1:T(2,128)}) %all-gather.11.cloned.1.call-update) | async-done | bytes 2359312 | tf_op jit(solution)/shard_map/all_gather | solution.py:28
  351.3 4.6 %fusion.25 = (f32[1,384,768]{2,0,1:T(1,128)S(1)}, f32[1,384,768]{2,0,1:T(1,128)S(1)}) fusion(f32[2,384,768]{2,0,1:T(2,128)} %all-gather.11.cloned.1.call-done), kind=kLoop, calls=%fused_computation.49 | loop fusion | bytes 4718592 | tf_op jit(solution)/shard_map/slice | solution.py:38
  356.0 0.2 broadcast_in_dim.11
  356.1 2.1 fusion.4
  358.3 4.0 %convolution_add_fusion = f32[512,768]{1,0:T(8,128)} fusion(f32[512,768]{1,0:T(8,128)S(1)} %convolution_add_fusion.1, f32[512,384]{0,1:T(8,128)S(1)} %fusion.4, f32[1,384,768]{2,0,1:T(1,128)S(1)} %get-tuple-element.5), kind=kOutput, calls=%fused_computation | convolution fusion | flops 1812332544 | bytes 5111808 | tf_op jit(solution)/shard_map/dot_general | solution.py:37
  (5 shorter events, 0.0 us)
Async XLA Ops:
  6.5 22.2 %copy-start.1 = (bf16[4,512,384]{2,1,0:T(8,128)(2,1)S(1)}, bf16[4,512,384]{2,1,0:T(8,128)(2,1)}, u32[]{:S(2)}) copy-start(bf16[4,512,384]{2,1,0:T(8,128)(2,1)} %param.8) | copy-start | bytes 4718596
  6.5 92.5 %all-gather.5.cloned.1.call-start = ((), (), s32[]{:S(2)}) async-start(), calls=%async_computation | async-start | bytes 2433024 | tf_op jit(solution)/shard_map/all_gather | solution.py:28
  8.2 175.0 %all-gather.7.cloned.1.call-start = ((), (), s32[]{:S(2)}) async-start(), calls=%async_computation.1 | async-start | bytes 2433024 | tf_op jit(solution)/shard_map/all_gather | solution.py:28
  8.2 5.9 %collective-permute-start = (f32[2,12,768]{2,0,1:T(2,128)}, f32[2,12,768]{2,0,1:T(2,128)S(1)}, u32[]{:S(2)}, u32[]{:S(2)}) collective-permute-start(f32[2,12,768]{2,0,1:T(2,128)} %pad_maximum_fusion.1), channel_id=1, source_target_pairs={{0,32},{32,64},{64,96},{96,128},{128,160},{160,192},{192,224},{224... | collective-permute-start | bytes 221192 | tf_op jit(solution)/shard_map/ppermute | solution.py:14
  14.8 252.5 %all-gather.9.cloned.1.call-start = ((), (), s32[]{:S(2)}) async-start(), calls=%async_computation.2 | async-start | bytes 2433024 | tf_op jit(solution)/shard_map/all_gather | solution.py:28
  14.9 6.4 %collective-permute-start.1 = (f32[2,12,768]{2,0,1:T(2,128)}, f32[2,12,768]{2,0,1:T(2,128)S(1)}, u32[]{:S(2)}, u32[]{:S(2)}) collective-permute-start(f32[2,12,768]{2,0,1:T(2,128)} %bitcast_select_fusion.1), channel_id=1, source_target_pairs={{0,32},{32,64},{64,96},{96,128},{128,160},{160,192},{192,224},{224... | collective-permute-start | bytes 221192 | tf_op jit(solution)/shard_map/ppermute | solution.py:14
  22.0 329.3 %all-gather.11.cloned.1.call-start = ((), (), s32[]{:S(2)}) async-start(), calls=%async_computation.3 | async-start | bytes 2433024 | tf_op jit(solution)/shard_map/all_gather | solution.py:28
  22.1 5.9 %collective-permute-start.2 = (f32[2,12,768]{2,0,1:T(2,128)}, f32[2,12,768]{2,0,1:T(2,128)S(1)}, u32[]{:S(2)}, u32[]{:S(2)}) collective-permute-start(f32[2,12,768]{2,0,1:T(2,128)} %bitcast_select_fusion), channel_id=1, source_target_pairs={{0,32},{32,64},{64,96},{96,128},{128,160},{160,192},{192,224},{224... | collective-permute-start | bytes 221192 | tf_op jit(solution)/shard_map/ppermute | solution.py:14
  28.7 0.7 copy-start.3
  99.0 4.7 %copy-start = (f32[512,768]{1,0:T(8,128)S(1)}, f32[512,768]{1,0:T(8,128)}, u32[]{:S(2)}) copy-start(f32[512,768]{1,0:T(8,128)} %param.7) | copy-start | bytes 4718596
  192.9 79.0 %copy-start.2 = (bf16[1,512,384]{1,2,0:T(8,128)(2,1)S(1)}, bf16[1,512,384]{1,2,0:T(8,128)(2,1)}, u32[]{:S(2)}) copy-start(bf16[1,512,384]{1,2,0:T(8,128)(2,1)} %copy.77) | copy-start | bytes 1179652
Sparse Core Ops, SparseCore 0:
  10.5 88.4 all-gather.4
  102.2 80.9 all-gather.6
  186.3 80.9 all-gather.8
  270.3 80.9 all-gather.10
where the time goes:
time: 369 us
  waiting for transfers between devices  301 us (82%)
  local copies, waits for them, and re-layouts  23.4 us (6%)
  matrix products  21.1 us (6%)
  between operations  13.3 us (4%)
  starting transfers between devices  5.89 us (2%)
  other arithmetic  3.75 us (1%)
    all_gather x4, waiting for transfers between devices, assimilate(): gathered = lax.all_gather(batch_pair, 'var', axis=1, tiled=True)  291 us
    slice x4, local copies, waits for them, and re-layouts, assimilate(): gathered[1]  17.9 us
    dot_general x4, matrix products, assimilate(): jnp.dot(weights, gathered[1], precision=lax.Precision.HIGHEST, preferred_...  12.4 us
    ppermute x3, waiting for transfers between devices, shifted(): return lax.ppermute(block, axis, route)  10.4 us
    dot_general x4, matrix products, assimilate(): lax.dot_general(state_rows, gathered[0], (((1,), (1,)), ((), ())), precis...  8.67 us
  transfers between devices with their start and end apart: 7, of which 7 were waited for; matrix products, arithmetic and copies ran while one was open for 10% of the time, Pallas kernels for 0%

commit v1 on v0

--- a/solution.py
+++ b/solution.py
@@ -25,7 +25,9 @@
 
 def assimilate(state_rows, taper_now, block_flags, batch_pair):
     localize = localizer(taper_now, block_flags)
-    gathered = lax.all_gather(batch_pair, "var", axis=1, tiled=True)
+    gathered = jnp.concatenate(
+        lax.all_to_all(jnp.stack([batch_pair] * lax.axis_size("var")), "var", 0, 0), axis=1
+    )
     covar = lax.dot_general(
         state_rows,
         gathered[0],

time: 369 us -> 299 us (0.81)
  the two profiles are of different devices: /device:TPU:8 before, /device:TPU:26 now
where the time goes in v1:
time: 299 us; the launch traced here: 294 us
  waiting for transfers between devices  150 us (50%)
  local copies, waits for them, and re-layouts  75.5 us (25%)
  starting transfers between devices  40 us (13%)
  matrix products  26.4 us (9%)
    all_to_all x4, waiting for transfers between devices, assimilate(): lax.all_to_all(jnp.stack([batch_pair] * lax.axis_size('var')), 'var', 0, 0)  141 us
    slice x4, local copies, waits for them, and re-layouts, assimilate(): gathered[1]  37.4 us
    all_to_all x4, starting transfers between devices, assimilate(): lax.all_to_all(jnp.stack([batch_pair] * lax.axis_size('var')), 'var', 0, 0)  34.2 us
    dot_general x4, matrix products, assimilate(): lax.dot_general(state_rows, gathered[0], (((1,), (1,)), ((), ())), precis...  14.1 us
    dot_general x4, matrix products, assimilate(): jnp.dot(weights, gathered[1], precision=lax.Precision.HIGHEST, preferred_...  12.3 us
    squeeze x4, local copies, waits for them, and re-layouts, assimilate(): gathered[0]  10.8 us
    another operation x4, local copies, waits for them, and re-layouts, assimilate(): jnp.stack([batch_pair] * lax.axis_size('var'))  9.04 us
    ppermute x3, waiting for transfers between devices, shifted(): return lax.ppermute(block, axis, route)  8.15 us
  transfers between devices with their start and end apart: 7, of which 6 were waited for; matrix products, arithmetic and copies ran while one was open for 24% of the time, Pallas kernels for 0%

profile of v1, /device:TPU:26, one launch (start us, length us, event | category | flops | bytes accessed | tf_op | source)
XLA Modules:
  0.0 293.7 jit_solution(13391390276890241191)
XLA Ops:
  0.0 0.8 copy_dynamic-update-slice_fusion.1
  0.8 0.8 copy_dynamic-update-slice_fusion
  1.5 0.1 copy.60
  1.6 2.0 stack.17
  3.6 13.6 %all-to-all-start = ((f32[32,2,12,768]{3,1,2,0:T(2,128)}), f32[32,2,12,768]{3,1,2,0:T(2,128)S(1)}, u32[]{:S(2)}, u32[]{:S(2)}) async-start(f32[32,2,12,768]{3,1,2,0:T(2,128)} %stack.17), calls=%async_computation | async-start | bytes 4718592 | tf_op jit(solution)/shard_map/all_to_all | solution.py:29
  17.2 1.9 collective-permute-start
  19.2 4.0 %collective-permute-done = f32[2,12,768]{2,1,0:T(8,128)S(1)} collective-permute-done((f32[2,12,768]{2,1,0:T(8,128)S(1)}, f32[2,12,768]{2,1,0:T(8,128)S(1)}, u32[]{:S(2)}, u32[]{:S(2)}) %collective-permute-start) | collective-permute-done | bytes 73760 | tf_op jit(solution)/shard_map/ppermute | solution.py:14
  23.2 0.1 copy.65
  23.3 48.6 %all-to-all-done = f32[32,2,12,768]{3,1,2,0:T(2,128)S(1)} async-done(((f32[32,2,12,768]{3,1,2,0:T(2,128)}), f32[32,2,12,768]{3,1,2,0:T(2,128)S(1)}, u32[]{:S(2)}, u32[]{:S(2)}) %all-to-all-start) | async-done | bytes 2359328 | tf_op jit(solution)/shard_map/all_to_all | solution.py:29
  71.9 2.0 stack.21
  73.9 6.5 %all-to-all-start.1 = ((f32[32,2,12,768]{3,1,2,0:T(2,128)}), f32[32,2,12,768]{3,1,2,0:T(2,128)}, u32[]{:S(2)}, u32[]{:S(2)}) async-start(f32[32,2,12,768]{3,1,2,0:T(2,128)} %stack.21), calls=%async_computation.1 | async-start | bytes 4718592 | tf_op jit(solution)/shard_map/all_to_all | solution.py:29
  80.5 1.9 collective-permute-start.1
  82.4 4.0 %collective-permute-done.1 = f32[2,12,768]{2,1,0:T(8,128)S(1)} collective-permute-done((f32[2,12,768]{2,1,0:T(8,128)S(1)}, f32[2,12,768]{2,1,0:T(8,128)S(1)}, u32[]{:S(2)}, u32[]{:S(2)}) %collective-permute-start.1) | collective-permute-done | bytes 73760 | tf_op jit(solution)/shard_map/ppermute | solution.py:14
  86.4 0.7 fusion.7
  87.1 1.0 copy.71
  88.0 46.9 %all-to-all-done.1 = f32[32,2,12,768]{3,1,2,0:T(2,128)} async-done(((f32[32,2,12,768]{3,1,2,0:T(2,128)}), f32[32,2,12,768]{3,1,2,0:T(2,128)}, u32[]{:S(2)}, u32[]{:S(2)}) %all-to-all-start.1) | async-done | bytes 2359328 | tf_op jit(solution)/shard_map/all_to_all | solution.py:29
  134.9 2.0 stack.22
  136.9 7.1 %all-to-all-start.2 = ((f32[32,2,12,768]{3,1,2,0:T(2,128)}), f32[32,2,12,768]{3,1,2,0:T(2,128)}, u32[]{:S(2)}, u32[]{:S(2)}) async-start(f32[32,2,12,768]{3,1,2,0:T(2,128)} %stack.22), calls=%async_computation.2 | async-start | bytes 4718592 | tf_op jit(solution)/shard_map/all_to_all | solution.py:29
  144.0 1.9 collective-permute-start.2
  146.0 2.3 fusion.13
  148.2 1.9 copy.89
  150.2 0.1 collective-permute-done.2
  150.3 0.9 fusion.12
  151.2 0.7 copy.76
  151.9 45.9 %all-to-all-done.2 = f32[32,2,12,768]{3,1,2,0:T(2,128)} async-done(((f32[32,2,12,768]{3,1,2,0:T(2,128)}), f32[32,2,12,768]{3,1,2,0:T(2,128)}, u32[]{:S(2)}, u32[]{:S(2)}) %all-to-all-start.2) | async-done | bytes 2359328 | tf_op jit(solution)/shard_map/all_to_all | solution.py:29
  197.9 3.0 %stack.23 = f32[32,2,12,768]{3,1,2,0:T(2,128)} broadcast(f32[2,12,768]{2,0,1:T(2,128)} %copy.76), dimensions={1,2,3} | broadcast | bytes 2433024 | tf_op jit(solution)/shard_map/stack | solution.py:29
  200.8 7.0 %all-to-all-start.3 = ((f32[32,2,12,768]{3,1,2,0:T(2,128)}), f32[32,2,12,768]{3,1,2,0:T(2,128)}, u32[]{:S(2)}, u32[]{:S(2)}) async-start(f32[32,2,12,768]{3,1,2,0:T(2,128)} %stack.23), calls=%async_computation.3 | async-start | bytes 4718592 | tf_op jit(solution)/shard_map/all_to_all | solution.py:29
  207.8 1.4 fusion.14
  209.3 0.1 copy.90
  209.4 0.1 copy.57
  209.5 1.0 copy.91
  210.4 0.1 copy.92
  210.5 0.1 copy.63
  210.6 0.9 copy.94
  211.6 0.1 copy.95
  211.7 0.1 copy.69
  211.8 0.2 copy.97
  212.0 0.8 copy.98
  212.7 0.1 copy.75
  212.8 7.4 %slice_reduce_fusion.6 = (f32[32,12,768]{2,1,0:T(8,128)}, f32[32,12,768]{2,1,0:T(8,128)}) fusion(f32[2,32,12,768]{3,0,2,1:T(2,128)S(1)} %bitcast.96), kind=kLoop, calls=%fused_computation.19 | loop fusion | bytes 4718592 | tf_op jit(solution)/shard_map/slice | solution.py:40
  220.2 2.7 squeeze.37
  223.0 1.1 squeeze.38
  224.2 0.2 broadcast_in_dim.8
  224.3 0.5 copy-done
  224.9 3.5 %fusion.1 = f32[512,384]{0,1:T(8,128)S(1)} fusion(f32[384,768]{1,0:T(8,128)} %squeeze.37, f32[512,768]{1,0:T(8,128)S(1)} %copy-done, f32[48,8,4,128]{3,2,1,0:T(4,128)S(1)} %bitcast.97, bf16[1,512,384]{1,2,0:T(8,128)(2,1)} %copy.89), kind=kOutput, calls=%fused_computation.9 | convolution fusion | flops 1812725760 | bytes 4718592 | tf_op jit(solution)/shard_map/dot_general | solution.py:31
  228.4 2.8 convolution_add_fusion.3
  231.2 10.0 %slice_reduce_fusion.4 = (f32[32,12,768]{2,1,0:T(8,128)S(1)}, f32[32,12,768]{2,1,0:T(8,128)}) fusion(f32[2,32,12,768]{3,0,2,1:T(2,128)} %bitcast.9), kind=kLoop, calls=%fused_computation.17 | loop fusion | bytes 4718592 | tf_op jit(solution)/shard_map/slice | solution.py:40
  241.2 2.9 squeeze.40
  244.1 1.1 squeeze.41
  245.2 0.2 broadcast_in_dim.9
  245.4 3.6 %fusion.2 = f32[512,384]{0,1:T(8,128)S(1)} fusion(f32[512,768]{1,0:T(8,128)S(1)} %convolution_add_fusion.3, f32[384,768]{1,0:T(8,128)} %squeeze.40, f32[48,8,4,128]{3,2,1,0:T(4,128)S(1)} %bitcast.98, bf16[1,512,384]{1,2,0:T(8,128)(2,1)} %copy.91), kind=kOutput, calls=%fused_computation.10 | convolution fusion | flops 1812725760 | bytes 4718592 | tf_op jit(solution)/shard_map/dot_general | solution.py:31
  249.0 2.8 convolution_add_fusion.2
  251.8 10.0 %slice_reduce_fusion.2 = (f32[32,12,768]{2,1,0:T(8,128)S(1)}, f32[32,12,768]{2,1,0:T(8,128)}) fusion(f32[2,32,12,768]{3,0,2,1:T(2,128)} %bitcast.13), kind=kLoop, calls=%fused_computation.15 | loop fusion | bytes 4718592 | tf_op jit(solution)/shard_map/slice | solution.py:40
  261.8 2.6 squeeze.43
  264.4 1.1 squeeze.44
  265.5 0.2 broadcast_in_dim.10
  265.7 3.6 %fusion.3 = f32[512,384]{0,1:T(8,128)S(1)} fusion(f32[512,768]{1,0:T(8,128)S(1)} %convolution_add_fusion.2, f32[384,768]{1,0:T(8,128)} %squeeze.43, f32[48,8,4,128]{3,2,1,0:T(4,128)S(1)} %bitcast.99, bf16[1,512,384]{1,2,0:T(8,128)(2,1)} %copy.94), kind=kOutput, calls=%fused_computation.11 | convolution fusion | flops 1812725760 | bytes 4718592 | tf_op jit(solution)/shard_map/dot_general | solution.py:31
  269.3 2.8 convolution_add_fusion.1
  272.1 10.0 %slice_reduce_fusion = (f32[32,12,768]{2,1,0:T(8,128)S(1)}, f32[32,12,768]{2,1,0:T(8,128)}) fusion(f32[2,32,12,768]{3,0,2,1:T(2,128)} %bitcast.17), kind=kLoop, calls=%fused_computation.13 | loop fusion | bytes 4718592 | tf_op jit(solution)/shard_map/slice | solution.py:40
  282.1 2.6 squeeze.46
  284.7 1.1 squeeze.47
  285.9 0.2 broadcast_in_dim.11
  286.1 3.5 %fusion.4 = f32[512,384]{0,1:T(8,128)S(1)} fusion(f32[512,768]{1,0:T(8,128)S(1)} %convolution_add_fusion.1, f32[384,768]{1,0:T(8,128)} %squeeze.46, f32[48,8,4,128]{3,2,1,0:T(4,128)S(1)} %bitcast.100, bf16[1,512,384]{1,2,0:T(8,128)(2,1)S(1)} %copy.97), kind=kOutput, calls=%fused_computation.12 | convolution fusion | flops 1812725760 | bytes 4718592 | tf_op jit(solution)/shard_map/dot_general | solution.py:31
  289.5 3.9 %convolution_add_fusion = f32[512,768]{1,0:T(8,128)} fusion(f32[512,768]{1,0:T(8,128)S(1)} %convolution_add_fusion.1, f32[512,384]{0,1:T(8,128)S(1)} %fusion.4, f32[384,768]{1,0:T(8,128)S(1)} %copy-done.4), kind=kOutput, calls=%fused_computation | convolution fusion | flops 1812332544 | bytes 5111808 | tf_op jit(solution)/shard_map/dot_general | solution.py:39
  (23 shorter events, 0.1 us)
Async XLA Ops:
  3.6 19.5 %copy-start.6 = (f32[3,12,768]{2,1,0:T(8,128)S(1)}, f32[3,12,768]{2,1,0:T(8,128)}, u32[]{:S(2)}) copy-start(f32[3,12,768]{2,1,0:T(8,128)} %param.12) | copy-start | bytes 331780
  3.6 19.5 %copy-start.7 = (f32[3,12,768]{2,1,0:T(8,128)S(1)}, f32[3,12,768]{2,1,0:T(8,128)}, u32[]{:S(2)}) copy-start(f32[3,12,768]{2,1,0:T(8,128)} %param.13) | copy-start | bytes 331780
  3.6 68.2 %all-to-all-start = ((f32[32,2,12,768]{3,1,2,0:T(2,128)}), f32[32,2,12,768]{3,1,2,0:T(2,128)S(1)}, u32[]{:S(2)}, u32[]{:S(2)}) async-start(f32[32,2,12,768]{3,1,2,0:T(2,128)} %stack.17), calls=%async_computation | async-start | bytes 4718592 | tf_op jit(solution)/shard_map/all_to_all | solution.py:29
  17.2 5.9 %collective-permute-start = (f32[2,12,768]{2,1,0:T(8,128)S(1)}, f32[2,12,768]{2,1,0:T(8,128)S(1)}, u32[]{:S(2)}, u32[]{:S(2)}) collective-permute-start(f32[2,12,768]{2,1,0:T(8,128)S(1)} %copy_dynamic-update-slice_fusion), channel_id=1, source_target_pairs={{0,32},{32,64},{64,96},{96,128},{128,160},{160,192},{192,224},{224... | collective-permute-start | bytes 221192 | tf_op jit(solution)/shard_map/ppermute | solution.py:14
  73.9 61.0 %all-to-all-start.1 = ((f32[32,2,12,768]{3,1,2,0:T(2,128)}), f32[32,2,12,768]{3,1,2,0:T(2,128)}, u32[]{:S(2)}, u32[]{:S(2)}) async-start(f32[32,2,12,768]{3,1,2,0:T(2,128)} %stack.21), calls=%async_computation.1 | async-start | bytes 4718592 | tf_op jit(solution)/shard_map/all_to_all | solution.py:29
  80.5 5.9 %collective-permute-start.1 = (f32[2,12,768]{2,1,0:T(8,128)S(1)}, f32[2,12,768]{2,1,0:T(8,128)S(1)}, u32[]{:S(2)}, u32[]{:S(2)}) collective-permute-start(f32[2,12,768]{2,1,0:T(8,128)S(1)} %fusion.10), channel_id=1, source_target_pairs={{0,32},{32,64},{64,96},{96,128},{128,160},{160,192},{192,224},{224... | collective-permute-start | bytes 221192 | tf_op jit(solution)/shard_map/ppermute | solution.py:14
  136.9 60.9 %all-to-all-start.2 = ((f32[32,2,12,768]{3,1,2,0:T(2,128)}), f32[32,2,12,768]{3,1,2,0:T(2,128)}, u32[]{:S(2)}, u32[]{:S(2)}) async-start(f32[32,2,12,768]{3,1,2,0:T(2,128)} %stack.22), calls=%async_computation.2 | async-start | bytes 4718592 | tf_op jit(solution)/shard_map/all_to_all | solution.py:29
  144.0 6.3 %collective-permute-start.2 = (f32[2,12,768]{2,1,0:T(8,128)}, f32[2,12,768]{2,1,0:T(8,128)}, u32[]{:S(2)}, u32[]{:S(2)}) collective-permute-start(f32[2,12,768]{2,1,0:T(8,128)} %fusion.7), channel_id=1, source_target_pairs={{0,32},{32,64},{64,96},{96,128},{128,160},{160,192},{192,224},{224... | collective-permute-start | bytes 221192 | tf_op jit(solution)/shard_map/ppermute | solution.py:14
  200.8 71.3 %all-to-all-start.3 = ((f32[32,2,12,768]{3,1,2,0:T(2,128)}), f32[32,2,12,768]{3,1,2,0:T(2,128)}, u32[]{:S(2)}, u32[]{:S(2)}) async-start(f32[32,2,12,768]{3,1,2,0:T(2,128)} %stack.23), calls=%async_computation.3 | async-start | bytes 4718592 | tf_op jit(solution)/shard_map/all_to_all | solution.py:29
  209.4 2.2 copy-start.8
  220.2 2.8 copy-start.1
  223.0 1.8 copy-start
  224.8 3.6 %copy-start.5 = (f32[384,768]{1,0:T(8,128)S(1)}, f32[384,768]{1,0:T(8,128)}, u32[]{:S(2)}) copy-start(f32[384,768]{1,0:T(8,128)} %squeeze.38) | copy-start | bytes 3538948
  245.4 3.6 %copy-start.2 = (f32[384,768]{1,0:T(8,128)S(1)}, f32[384,768]{1,0:T(8,128)}, u32[]{:S(2)}) copy-start(f32[384,768]{1,0:T(8,128)} %squeeze.41) | copy-start | bytes 3538948
  265.7 3.6 %copy-start.3 = (f32[384,768]{1,0:T(8,128)S(1)}, f32[384,768]{1,0:T(8,128)}, u32[]{:S(2)}) copy-start(f32[384,768]{1,0:T(8,128)} %squeeze.44) | copy-start | bytes 3538948
  286.0 3.5 %copy-start.4 = (f32[384,768]{1,0:T(8,128)S(1)}, f32[384,768]{1,0:T(8,128)}, u32[]{:S(2)}) copy-start(f32[384,768]{1,0:T(8,128)} %squeeze.47) | copy-start | bytes 3538948
